TPU v7x, 256 devices: a whole 4x4x8 slice. The times are simulated.
256 devices in a mesh: expert: 32 (over x, y, core), shard: 8 (over z).
Axes of the slice: x: 4, y: 4, z: 8, core: 2. Of those that a mesh axis runs over, the one named last changes fastest.
Arguments:
- head_outputs: bfloat16 [32768, 1024], P(('expert', 'shard')), may hold values from -6 to 6
- residual: bfloat16 [32768, 1024], P(('expert', 'shard')), may hold values from -4 to 4
- output_weight: bfloat16 [1024, 1024], P('shard'), may hold values from -0.1875 to 0.1875
- router: bfloat16 [1024, 32], replicated, may hold values from -0.095703125 to 0.095703125
- norm_gain: float32 [1024], replicated, may hold values from 0.1 to 1.9
- placed_gate_up: bfloat16 [64, 1024, 1024], P('expert', 'shard'), may hold values from -0.1875 to 0.1875
- placed_down: bfloat16 [64, 512, 1024], P('expert', 'shard'), may hold values from -0.25 to 0.25
- routes: int32 [32768, 8], P(('expert', 'shard')), may hold values from 0 to 31, all different within a row; in each aligned block of 128 rows (0 to 127, 128 to 255, ...) at most 48 rows name the same one
- replica_pick: int32 [32768, 8], P(('expert', 'shard')), may hold values from 0 to 5
- placement: int32 [64], replicated, may hold values from 0 to 31, as said below
- final_gain: float32 [1024], replicated, may hold values from 0.1 to 1.9
Outputs:
- next_input: bfloat16 [32768, 1024], P(('expert', 'shard'))
Inputs may be any that keep to these rules, and one draw needn't show every extreme that they name: `routes`: each token names 8 different experts. Among the 128 tokens of one device no expert is named more than 48 times, and in some device's tokens one expert is named exactly 48 times. `placement`: every expert holds one to three of the 64 placements: a quarter of the experts hold three, half of them two, the rest one.
All inputs are finite; a program needn't handle non-finite values.
Results may differ from a plain program's by a relative error of at most 0.011.
Values may be sent and summed in bfloat16 or wider, within the bound.
A program may use at most 128 MiB of HBM per device.

v0:
```python
import math

import jax
import jax.numpy as jnp
from jax import lax
from jax.sharding import PartitionSpec as P

CAP = 48


eps_norm = 1e-06
most_copies = 3


def rms_scale(values, scale_gain):
    mean_square = jnp.mean(values * values, axis=-1, keepdims=True)
    return values * lax.rsqrt(mean_square + eps_norm) * scale_gain


def choose_slots(routes, replica_pick, placement, experts):
    labels = jnp.arange(experts, dtype=jnp.int32)
    holder_mask = (placement[None, :] == labels[:, None]).astype(jnp.int32)
    before = jnp.cumsum(holder_mask, axis=1) - holder_mask
    copies = jnp.sum(holder_mask, axis=1)
    places = jnp.arange(placement.shape[0], dtype=jnp.int32)
    route_hits = (routes[..., None] == labels).astype(jnp.int32)
    held_count = jnp.sum(route_hits * copies, axis=-1)
    wanted = replica_pick % held_count
    chosen = jnp.zeros(routes.shape, jnp.int32)
    for replica in range(most_copies):
        column = jnp.sum(
            holder_mask * (before == replica).astype(jnp.int32) * places[None, :], axis=1
        )
        candidate = jnp.sum(route_hits * column, axis=-1)
        chosen = jnp.where(wanted == replica, candidate, chosen)
    return chosen


def padded_experts(inbound, gate_up, down_proj):
    sources, slot_count, slot_depth, model_width = inbound.shape
    per_source = slot_count * slot_depth
    upper_bound = max(1, 1024 // per_source)
    power_two = 1 << upper_bound.bit_length() - 1
    group_size = math.gcd(sources, power_two)
    stacked = inbound.reshape(
        sources // group_size, group_size, slot_count, slot_depth, model_width
    )
    hidden_units = down_proj.shape[1]

    def apply_block(block_part):
        both_parts = jnp.einsum(
            "bjmd,jdf->bjmf", block_part, gate_up, preferred_element_type=jnp.float32
        )
        activated = (
            jax.nn.silu(both_parts[..., :hidden_units]) * both_parts[..., hidden_units:]
        ).astype(jnp.bfloat16)
        return jnp.einsum(
            "bjmf,jfd->bjmd", activated, down_proj, preferred_element_type=jnp.float32
        ).astype(jnp.bfloat16)

    return lax.map(apply_block, stacked).reshape(inbound.shape)


def body(
    head_outputs,
    residual,
    output_weight,
    router,
    norm_gain,
    placed_gate_up,
    placed_down,
    routes,
    replica_pick,
    placement,
    final_gain,
):
    row_count, model_width = residual.shape
    route_count = routes.shape[1]
    experts = router.shape[1]
    place_count = placement.shape[0]
    groups = lax.axis_size("expert")
    slot_count = place_count // groups
    capacity = CAP
    projected = jnp.dot(
        head_outputs,
        lax.all_gather(output_weight, "shard", axis=0, tiled=True),
        preferred_element_type=jnp.float32,
    )
    hidden = (residual.astype(jnp.float32) + projected).astype(jnp.bfloat16)
    hidden_wide = hidden.astype(jnp.float32)
    normed = rms_scale(hidden_wide, norm_gain).astype(jnp.bfloat16)
    logits = jnp.dot(normed, router, preferred_element_type=jnp.float32)
    labels = jnp.arange(experts, dtype=jnp.int32)
    selector = (routes[..., None] == labels).astype(jnp.float32)
    chosen_logits = jnp.sum(selector * logits[:, None, :], axis=-1)
    raised = jnp.exp(chosen_logits)
    route_weight = raised / jnp.sum(raised, axis=-1, keepdims=True)
    slot_ids = choose_slots(routes, replica_pick, placement, experts).reshape(-1)
    slot_hits = (slot_ids[:, None] == jnp.arange(place_count, dtype=jnp.int32)).astype(jnp.int32)
    slot_rank = jnp.sum((jnp.cumsum(slot_hits, axis=0) - slot_hits) * slot_hits, axis=1)
    copies_out = jnp.repeat(normed, route_count, axis=0)
    gate_up, down_proj = (
        lax.all_gather(placed_gate_up, "shard", axis=1, tiled=True),
        lax.all_gather(placed_down, "shard", axis=1, tiled=True),
    )
    buffer_index = slot_ids * capacity + slot_rank
    outbound = (
        jnp.zeros((place_count * capacity, model_width), jnp.bfloat16)
        .at[buffer_index]
        .set(copies_out)
    )
    inbound = lax.all_to_all(
        outbound.reshape(groups, slot_count * capacity, model_width),
        "expert",
        split_axis=0,
        concat_axis=0,
        tiled=True,
    )
    inbound = inbound.reshape(groups, slot_count, capacity, model_width)
    answers = padded_experts(inbound, gate_up, down_proj)
    returned = lax.all_to_all(
        answers.reshape(groups, slot_count * capacity, model_width),
        "expert",
        split_axis=0,
        concat_axis=0,
        tiled=True,
    )
    returned = returned.reshape(place_count * capacity, model_width)
    gathered = returned[buffer_index].reshape(row_count, route_count, model_width)
    mixture = jnp.sum(route_weight[..., None] * gathered.astype(jnp.float32), axis=1)
    return rms_scale(hidden_wide + mixture, final_gain).astype(jnp.bfloat16)


def solution(mesh):
    return jax.shard_map(
        body,
        mesh=mesh,
        in_specs=(
            P(("expert", "shard"), None),
            P(("expert", "shard"), None),
            P("shard", None),
            P(),
            P(),
            P("expert", "shard", None),
            P("expert", "shard", None),
            P(("expert", "shard"), None),
            P(("expert", "shard"), None),
            P(),
            P(),
        ),
        out_specs=P(("expert", "shard"), None),
        check_vma=False,
    )
```

profile of v0, /device:TPU:8, one launch (start us, length us, event | category | flops | bytes accessed | tf_op | source)
XLA Modules:
  0.0 298.7 jit_solution(8808641445974317560)
XLA Ops:
  6.5 0.7 all-gather.4.cloned.1.call-update
  7.3 0.7 all-gather.8.cloned.1.call-update
  8.1 0.7 all-gather.6.cloned.1.call-update
  9.6 0.8 fusion.33
  10.4 0.8 select_reduce_fusion.3
  11.3 0.8 broadcast_multiply_fusion
  12.6 18.0 %reduce-window.6 = s32[64,8,128]{2,1,0:T(8,128)S(1)} reduce-window(s32[64,8,128]{2,1,0:T(8,128)S(1)} %fusion.27, s32[]{:T(128)} %copy.53), window={size=1x1x128 pad=0_0x0_0x127_0}, to_apply=%region_12.13 | reduce-window | flops 8323072 | bytes 524292 | tf_op jit(solution)/shard_map/reduce-window
  31.3 21.6 %all-gather.4.cloned.1.call-done = bf16[1024,1024]{1,0:T(8,128)(2,1)} async-done(((bf16[128,1024]{1,0:T(8,128)(2,1)}), bf16[1024,1024]{1,0:T(8,128)(2,1)}) %all-gather.4.cloned.1.call-update) | async-done | bytes 2097168 | tf_op jit(solution)/shard_map/all_gather | solution.py:86
  52.9 2.1 multiply_reduce_fusion.1
  55.2 9.0 %scatter_custom_fusion = bf16[3072,1024]{1,0:T(8,128)(2,1)} fusion(s32[1024]{0:T(1024)S(1)} %bitcast.75, bf16[]{:T(256)} %constant.52.clone.1, bf16[128,1024]{1,0:T(8,128)(2,1)S(1)} %multiply_convert_fusion.1), kind=kCustom, calls=%fused_computation.18 | custom fusion | bytes 6553602 | tf_op jit(solution)/shard_map/scatter | solution.py:110
  64.2 8.2 %all-to-all-start = ((bf16[32,96,1024]{2,1,0:T(8,128)(2,1)}), bf16[32,96,1024]{2,1,0:T(8,128)(2,1)}, u32[]{:S(2)}, u32[]{:S(2)}) async-start(bf16[32,96,1024]{2,1,0:T(8,128)(2,1)} %bitcast.70), calls=%async_computation | async-start | bytes 12582912 | tf_op jit(solution)/shard_map/all_to_all | solution.py:112
  72.4 22.6 %all-gather.8.cloned.1.call-done = bf16[2,512,1024]{2,1,0:T(8,128)(2,1)} async-done(((bf16[2,64,1024]{2,1,0:T(8,128)(2,1)}), bf16[2,512,1024]{2,1,0:T(8,128)(2,1)}) %all-gather.8.cloned.1.call-update) | async-done | bytes 2097168 | tf_op jit(solution)/shard_map/all_gather | solution.py:104
  95.0 55.0 %all-gather.6.cloned.1.call-done = bf16[2,1024,1024]{2,1,0:T(8,128)(2,1)} async-done(((bf16[2,128,1024]{2,1,0:T(8,128)(2,1)}), bf16[2,1024,1024]{2,1,0:T(8,128)(2,1)}) %all-gather.6.cloned.1.call-update) | async-done | bytes 4194320 | tf_op jit(solution)/shard_map/all_gather | solution.py:103
  150.1 9.9 %all-to-all-done = bf16[32,96,1024]{2,1,0:T(8,128)(2,1)} async-done(((bf16[32,96,1024]{2,1,0:T(8,128)(2,1)}), bf16[32,96,1024]{2,1,0:T(8,128)(2,1)}, u32[]{:S(2)}, u32[]{:S(2)}) %all-to-all-start) | async-done | bytes 6291488 | tf_op jit(solution)/shard_map/all_to_all | solution.py:112
  160.0 27.9 %while.10 = (s32[]{:T(128)}, bf16[4,8,2,48,1024]{4,3,2,1,0:T(8,128)(2,1)}, bf16[4,8,2,48,1024]{4,3,2,1,0:T(8,128)(2,1)}, bf16[2,1024,1024]{2,1,0:T(8,128)(2,1)}, bf16[2,512,1024]{2,1,0:T(8,128)(2,1)}, /*index=5*/s32[]{:T(128)}) while((s32[]{:T(128)}, bf16[4,8,2,48,1024]{4,3,2,1,0:T(8,128)(2,1)}, bf16[4,8,2,48,1024]{4,3,2,1,0:T(8,128)(2,1)}, ...), condition=%wide.region_17.18_spmd, body=%wide.region_16.17_spmd.sunk | while | flops 2419064832 | bytes 27263088 | solution.py:61
  160.0 4.6 %fusion.48 = f32[8,2,48,1024]{3,2,0,1:T(8,128)S(1)} fusion(bf16[2,1024,1024]{2,1,0:T(8,128)(2,1)} %get-tuple-element.113, bf16[4,8,2,48,1024]{4,3,2,1,0:T(8,128)(2,1)} %get-tuple-element.112, s32[]{:T(128)S(6)} %copy.48), kind=kOutput, calls=%fused_computation.6.clone.1 | convolution fusion | flops 1610612736 | bytes 8912900 | tf_op jit(solution)/shard_map/while/body/eval_jaxpr/bjmd,jdf->bjmf/dot_general | solution.py:51
  164.6 1.0 fusion.49
  165.6 1.3 copy_dynamic-update-slice_fusion.2
  166.9 4.6 %fusion.48 = f32[8,2,48,1024]{3,2,0,1:T(8,128)S(1)} fusion(bf16[2,1024,1024]{2,1,0:T(8,128)(2,1)} %get-tuple-element.113, bf16[4,8,2,48,1024]{4,3,2,1,0:T(8,128)(2,1)} %get-tuple-element.112, s32[]{:T(128)S(6)} %copy.48), kind=kOutput, calls=%fused_computation.6.clone.1 | convolution fusion | flops 1610612736 | bytes 8912900 | tf_op jit(solution)/shard_map/while/body/eval_jaxpr/bjmd,jdf->bjmf/dot_general | solution.py:51
  171.6 1.0 fusion.49
  172.6 1.4 copy_dynamic-update-slice_fusion.2
  174.0 4.6 %fusion.48 = f32[8,2,48,1024]{3,2,0,1:T(8,128)S(1)} fusion(bf16[2,1024,1024]{2,1,0:T(8,128)(2,1)} %get-tuple-element.113, bf16[4,8,2,48,1024]{4,3,2,1,0:T(8,128)(2,1)} %get-tuple-element.112, s32[]{:T(128)S(6)} %copy.48), kind=kOutput, calls=%fused_computation.6.clone.1 | convolution fusion | flops 1610612736 | bytes 8912900 | tf_op jit(solution)/shard_map/while/body/eval_jaxpr/bjmd,jdf->bjmf/dot_general | solution.py:51
  178.6 1.0 fusion.49
  179.7 1.3 copy_dynamic-update-slice_fusion.2
  181.0 4.6 %fusion.48 = f32[8,2,48,1024]{3,2,0,1:T(8,128)S(1)} fusion(bf16[2,1024,1024]{2,1,0:T(8,128)(2,1)} %get-tuple-element.113, bf16[4,8,2,48,1024]{4,3,2,1,0:T(8,128)(2,1)} %get-tuple-element.112, s32[]{:T(128)S(6)} %copy.48), kind=kOutput, calls=%fused_computation.6.clone.1 | convolution fusion | flops 1610612736 | bytes 8912900 | tf_op jit(solution)/shard_map/while/body/eval_jaxpr/bjmd,jdf->bjmf/dot_general | solution.py:51
  185.6 1.0 fusion.49
  186.6 1.3 copy_dynamic-update-slice_fusion.2
  187.9 5.1 %all-to-all-start.1 = ((bf16[32,96,1024]{2,1,0:T(8,128)(2,1)}), bf16[32,96,1024]{2,1,0:T(8,128)(2,1)}, u32[]{:S(2)}, u32[]{:S(2)}) async-start(bf16[32,96,1024]{2,1,0:T(8,128)(2,1)} %bitcast.71), calls=%async_computation.1 | async-start | bytes 12582912 | tf_op jit(solution)/shard_map/all_to_all | solution.py:121
  193.5 87.8 %all-to-all-done.1 = bf16[32,96,1024]{2,1,0:T(8,128)(2,1)} async-done(((bf16[32,96,1024]{2,1,0:T(8,128)(2,1)}), bf16[32,96,1024]{2,1,0:T(8,128)(2,1)}, u32[]{:S(2)}, u32[]{:S(2)}) %all-to-all-start.1) | async-done | bytes 6291488 | tf_op jit(solution)/shard_map/all_to_all | solution.py:121
  281.3 8.6 %gather_fusion = bf16[1024,1024]{1,0:T(8,128)(2,1)S(1)} fusion(bf16[3072,1024]{1,0:T(8,128)(2,1)} %bitcast.16, s32[1024]{0:T(1024)S(1)} %broadcast_clamp_fusion), kind=kCustom, calls=%fused_computation | custom fusion | bytes 4198400 | tf_op jit(solution)/shard_map/gather | solution.py:129
  289.9 1.3 fusion.17
  291.3 0.8 multiply_convert_fusion
  (50 shorter events, 2.8 us)
Async XLA Ops:
  6.5 46.4 %copy-start = (bf16[128,1024]{1,0:T(8,128)(2,1)S(1)}, bf16[128,1024]{1,0:T(8,128)(2,1)}, u32[]{:S(2)}) copy-start(bf16[128,1024]{1,0:T(8,128)(2,1)} %param.13) | copy-start | bytes 786436
  6.5 46.4 %copy-start.1 = (bf16[128,1024]{1,0:T(8,128)(2,1)S(1)}, bf16[128,1024]{1,0:T(8,128)(2,1)}, u32[]{:S(2)}) copy-start(bf16[128,1024]{1,0:T(8,128)(2,1)} %param.14) | copy-start | bytes 786436
  6.5 46.4 %all-gather.4.cloned.1.call-start = ((), (), s32[]{:S(2)}) async-start(), calls=%async_computation.2 | async-start | bytes 2359296 | tf_op jit(solution)/shard_map/all_gather | solution.py:86
  7.3 87.8 %all-gather.8.cloned.1.call-start = ((), (), s32[]{:S(2)}) async-start(), calls=%async_computation.4 | async-start | bytes 2359296 | tf_op jit(solution)/shard_map/all_gather | solution.py:104
  8.0 142.1 %all-gather.6.cloned.1.call-start = ((), (), s32[]{:S(2)}) async-start(), calls=%async_computation.3 | async-start | bytes 4718592 | tf_op jit(solution)/shard_map/all_gather | solution.py:103
  30.7 24.3 %copy-start.4 = (f32[1024]{0:T(1024)S(1)}, f32[1024]{0:T(1024)}, u32[]{:S(2)}) copy-start(f32[1024]{0:T(1024)} %param.17) | copy-start | bytes 12292
  64.2 95.8 %all-to-all-start = ((bf16[32,96,1024]{2,1,0:T(8,128)(2,1)}), bf16[32,96,1024]{2,1,0:T(8,128)(2,1)}, u32[]{:S(2)}, u32[]{:S(2)}) async-start(bf16[32,96,1024]{2,1,0:T(8,128)(2,1)} %bitcast.70), calls=%async_computation | async-start | bytes 12582912 | tf_op jit(solution)/shard_map/all_to_all | solution.py:112
  160.0 4.6 %copy-start.6 = (bf16[2,512,1024]{2,1,0:T(8,128)(2,1)S(1)}, bf16[2,512,1024]{2,1,0:T(8,128)(2,1)}, u32[]{:S(2)}) copy-start(bf16[2,512,1024]{2,1,0:T(8,128)(2,1)} %get-tuple-element.114) | copy-start | bytes 6291460 | tf_op jit(solution)/shard_map/while
  166.9 4.6 %copy-start.6 = (bf16[2,512,1024]{2,1,0:T(8,128)(2,1)S(1)}, bf16[2,512,1024]{2,1,0:T(8,128)(2,1)}, u32[]{:S(2)}) copy-start(bf16[2,512,1024]{2,1,0:T(8,128)(2,1)} %get-tuple-element.114) | copy-start | bytes 6291460 | tf_op jit(solution)/shard_map/while
  174.0 4.6 %copy-start.6 = (bf16[2,512,1024]{2,1,0:T(8,128)(2,1)S(1)}, bf16[2,512,1024]{2,1,0:T(8,128)(2,1)}, u32[]{:S(2)}) copy-start(bf16[2,512,1024]{2,1,0:T(8,128)(2,1)} %get-tuple-element.114) | copy-start | bytes 6291460 | tf_op jit(solution)/shard_map/while
  181.0 4.6 %copy-start.6 = (bf16[2,512,1024]{2,1,0:T(8,128)(2,1)S(1)}, bf16[2,512,1024]{2,1,0:T(8,128)(2,1)}, u32[]{:S(2)}) copy-start(bf16[2,512,1024]{2,1,0:T(8,128)(2,1)} %get-tuple-element.114) | copy-start | bytes 6291460 | tf_op jit(solution)/shard_map/while
  187.9 5.1 %copy-start.2 = (bf16[1024,32]{0,1:T(8,128)(2,1)S(1)}, bf16[1024,32]{0,1:T(8,128)(2,1)}, u32[]{:S(2)}) copy-start(bf16[1024,32]{0,1:T(8,128)(2,1)} %param.16) | copy-start | bytes 196612
  187.9 5.3 %copy-start.3 = (s32[128,8]{0,1:T(8,128)S(1)}, s32[128,8]{0,1:T(8,128)}, u32[]{:S(2)}) copy-start(s32[128,8]{0,1:T(8,128)} %param.20) | copy-start | bytes 12292
  187.9 93.4 %all-to-all-start.1 = ((bf16[32,96,1024]{2,1,0:T(8,128)(2,1)}), bf16[32,96,1024]{2,1,0:T(8,128)(2,1)}, u32[]{:S(2)}, u32[]{:S(2)}) async-start(bf16[32,96,1024]{2,1,0:T(8,128)(2,1)} %bitcast.71), calls=%async_computation.1 | async-start | bytes 12582912 | tf_op jit(solution)/shard_map/all_to_all | solution.py:121
  289.9 1.5 copy-start.5
Sparse Core Ops, SparseCore 0:
  9.2 43.6 all-gather.3
  54.7 40.2 all-gather.7
  96.8 53.1 all-gather.5
where the time goes:
time: 299 us
  waiting for transfers between devices  199 us (67%)
  matrix products  24.8 us (8%)
  other arithmetic  24.1 us (8%)
  local copies, waits for them, and re-layouts  23.9 us (8%)
  starting transfers between devices  13.4 us (4%)
  between operations  13.3 us (4%)
    all_to_all x1, waiting for transfers between devices, body(): lax.all_to_all(answers.reshape(groups, slot_count * capacity, model_width...  87.8 us
    all_gather x1, waiting for transfers between devices, body(): lax.all_gather(placed_gate_up, 'shard', axis=1, tiled=True)  55 us
    all_gather x1, waiting for transfers between devices, body(): lax.all_gather(placed_down, 'shard', axis=1, tiled=True)  22.6 us
    all_gather x1, waiting for transfers between devices, body(): lax.all_gather(output_weight, 'shard', axis=0, tiled=True)  21.6 us
    dot_general x4, matrix products, apply_block(): jnp.einsum('bjmd,jdf->bjmf', block_part, gate_up, preferred_element_type=...  18.4 us
    another operation x3, other arithmetic  18.2 us
    all_to_all x1, waiting for transfers between devices, body(): lax.all_to_all(outbound.reshape(groups, slot_count * capacity, model_widt...  9.92 us
    scatter x1, local copies, waits for them, and re-layouts, body(): outbound = jnp.zeros((place_count * capacity, model_width), jnp.bfloat16)...  9.04 us
  transfers between devices with their start and end apart: 5, of which 5 were waited for; matrix products, arithmetic and copies ran while one was open for 11% of the time, Pallas kernels for 0%

commit v1 on v0

v1 whole, which is shorter than its diff:
```python
import functools

import jax
import jax.numpy as jnp
from jax import lax
from jax.experimental import pallas as pl
from jax.experimental.pallas import tpu as pltpu
from jax.sharding import PartitionSpec as P

NX, NY, NZ = 4, 4, 8
CHIPS = NX * NY
D = 1024
FF = 512
EXPERTS = 32
TOP = 8
TOK = 128
CAP = 48
PL = 64
QW = 256
HALF = FF // 2
SLOTS = 4
ROWS = CHIPS * CAP
EPS = 1e-06
MESH = pl.DeviceIdType.MESH
BF = jnp.bfloat16
F32 = jnp.float32
ZHOPS = ((4, 3), (3, 4))
PHOPS = ((2, 1), (1, 2))
NT = (((1,), (1,)), ((), ()))
TN = (((0,), (0,)), ((), ()))


def wrap(v, n):
    return lax.rem(v + n, n)


def rms(values, gain):
    mean_square = jnp.mean(values * values, axis=-1, keepdims=True)
    return values * lax.rsqrt(mean_square + EPS) * gain


def body_kernel(
    ho,
    res,
    wo_in,
    gu_in,
    dn_in,
    router,
    ngain,
    fgain,
    routes,
    pick,
    plc,
    out_ref,
    ho_v,
    res_v,
    wo,
    wgu,
    wd,
    xq,
    xc,
    act,
    yc,
    part,
    rb1,
    rb2,
    hid,
    wt,
    pw,
    lsem,
    o_r,
    o_s,
    op_r,
    op_s,
    z_r,
    z_s,
    zp_r,
    zp_s,
    a1_r,
    a1_s,
    a2_r,
    a2_s,
    r1_r,
    r1_s,
    r2_r,
    r2_s,
):
    e = lax.axis_index("expert")
    z = lax.axis_index("shard")
    chip = lax.div(e, 2)
    core = lax.rem(e, 2)
    x = lax.div(chip, NY)
    y = lax.rem(chip, NY)

    def dev(xx, yy, zz, cc):
        return ((xx * NY + yy) * 2 + cc, zz)

    partner = dev(x, y, z, 1 - core)
    znb = (dev(x, y, wrap(z + 1, NZ), core), dev(x, y, wrap(z - 1, NZ), core))
    xnb = (dev(wrap(x + 1, NX), y, z, core), dev(wrap(x - 1, NX), y, z, core))
    ynb = (dev(x, wrap(y + 1, NY), z, core), dev(x, wrap(y - 1, NY), z, core))

    sends = []

    def send(src, dst, ssem, rsem, to):
        copy = pltpu.make_async_remote_copy(
            src_ref=src, dst_ref=dst, send_sem=ssem, recv_sem=rsem, device_id=to, device_id_type=MESH
        )
        copy.start()
        sends.append(copy)

    def arrived(dst, ssem, rsem):
        pltpu.make_async_remote_copy(
            src_ref=dst, dst_ref=dst, send_sem=ssem, recv_sem=rsem, device_id=partner, device_id_type=MESH
        ).wait_recv()

    zrow = pl.ds(pl.multiple_of(z * 128, 128), 128)
    zrow2 = pl.ds(pl.multiple_of(z * 64, 64), 64)
    local = []

    def load(src, dst):
        copy = pltpu.make_async_copy(src, dst, lsem.at[len(local)])
        copy.start()
        local.append(copy)

    for q in range(4):
        load(wo_in.at[:, pl.ds(q * QW, QW)], wo.at[q, zrow, :])
    load(ho, ho_v)
    load(res, res_v)
    for c in range(2):
        for j in range(2):
            s = 2 * core + j
            load(gu_in.at[j, :, pl.ds(c * HALF, HALF)], wgu.at[c, s, zrow, pl.ds(0, HALF)])
            load(gu_in.at[j, :, pl.ds(FF + c * HALF, HALF)], wgu.at[c, s, zrow, pl.ds(HALF, HALF)])
    for j in range(2):
        load(dn_in.at[j], wd.at[2 * core + j, zrow2, :])

    barrier = pltpu.get_barrier_semaphore()
    for nb in (partner,) + znb + xnb + ynb:
        pl.semaphore_signal(barrier, inc=1, device_id=nb, device_id_type=MESH)
    pl.semaphore_wait(barrier, 7)

    for copy in local:
        copy.wait()

    def shard_of(dirn, k):
        return wrap(z - k, NZ) if dirn == 0 else wrap(z + k, NZ)

    class Ring:
        def __init__(self, where, hops, s_sem, r_sem, ps_sem, pr_sem, share_own):
            self.where, self.hops = where, hops
            self.s_sem, self.r_sem, self.ps_sem, self.pr_sem = s_sem, r_sem, ps_sem, pr_sem
            self.share_own = share_own

        def go(self, dirn, k):
            at = self.where(core, shard_of(dirn, k))
            i = dirn * 4 + k
            send(at, at, self.s_sem(i), self.r_sem(i), znb[dirn])

        def begin(self):
            self.go(0, 0)
            self.go(1, 0)
            if self.share_own:
                at = self.where(core, z)
                send(at, at, self.ps_sem(8), self.pr_sem(8), partner)

        def arrive(self, k):
            for dirn in range(2):
                if k < self.hops[dirn]:
                    i = dirn * 4 + k
                    at = self.where(core, shard_of(dirn, k + 1))
                    arrived(at, self.s_sem(i), self.r_sem(i))
                    if k + 1 < self.hops[dirn]:
                        self.go(dirn, k + 1)
                    send(at, at, self.ps_sem(i), self.pr_sem(i), partner)

        def from_partner(self):
            other = 1 - core
            for dirn in range(2):
                for k in range(self.hops[dirn]):
                    i = dirn * 4 + k
                    arrived(self.where(other, shard_of(dirn, k + 1)), self.ps_sem(i), self.pr_sem(i))
            if self.share_own:
                arrived(self.where(other, z), self.ps_sem(8), self.pr_sem(8))

    def wo_at(i):
        return lambda cc, zz: wo.at[2 * cc + i, pl.ds(pl.multiple_of(zz * 128, 128), 128), :]

    def gu_at(c, j):
        return lambda cc, zz: wgu.at[c, 2 * cc + j, pl.ds(pl.multiple_of(zz * 128, 128), 128), :]

    def dn_at(j):
        return lambda cc, zz: wd.at[2 * cc + j, pl.ds(pl.multiple_of(zz * 64, 64), 64), :]

    def sem_row(ref, u):
        return lambda i: ref.at[u, i]

    def ring(where, u, hops, refs, own):
        return Ring(where, hops, *[sem_row(r, u) for r in refs], own)

    orings = [ring(wo_at(i), i, ZHOPS[i], (o_s, o_r, op_s, op_r), False) for i in range(2)]
    zrefs = (z_s, z_r, zp_s, zp_r)
    pieces = [
        [ring(gu_at(0, j), j, ZHOPS[j], zrefs, True) for j in range(2)],
        [ring(dn_at(j), 2 + j, ZHOPS[j], zrefs, True) for j in range(2)],
        [ring(gu_at(1, j), 4 + j, ZHOPS[j], zrefs, True) for j in range(2)],
    ]

    def z_begin(p):
        for r in pieces[p]:
            r.begin()

    def z_arrive(p, k):
        for r in pieces[p]:
            r.arrive(k)

    zqueue = [
        lambda: z_arrive(0, 0),
        lambda: z_arrive(1, 0),
        lambda: (z_arrive(0, 1), z_begin(2)),
        lambda: z_arrive(1, 1),
        lambda: z_arrive(0, 2),
        lambda: z_arrive(2, 0),
        lambda: z_arrive(1, 2),
        lambda: z_arrive(0, 3),
        lambda: z_arrive(2, 1),
        lambda: z_arrive(1, 3),
        lambda: z_arrive(2, 2),
        lambda: z_arrive(2, 3),
    ]

    def pump():
        if zqueue:
            zqueue.pop(0)()

    for r in orings:
        r.begin()
    for k in range(3):
        for r in orings:
            r.arrive(k)
    z_begin(0)
    z_begin(1)

    plc_row = plc[...].astype(F32)
    rows64 = lax.broadcasted_iota(jnp.int32, (PL, PL), 0)
    cols64 = lax.broadcasted_iota(jnp.int32, (PL, PL), 1)
    plc_col = jnp.sum(jnp.where(rows64 == cols64, plc_row, 0.0), axis=1, keepdims=True)
    same = plc_col == plc_row
    copies = jnp.sum(jnp.where(same, 1.0, 0.0), axis=1, keepdims=True)
    order = jnp.sum(jnp.where(same & (cols64 < rows64), 1.0, 0.0), axis=1, keepdims=True)
    eye8 = (
        lax.broadcasted_iota(jnp.int32, (TOP, TOP), 0) == lax.broadcasted_iota(jnp.int32, (TOP, TOP), 1)
    ).astype(BF)
    routes_t = lax.dot_general(eye8, routes[...].astype(BF), NT, preferred_element_type=F32)
    pick_t = lax.dot_general(eye8, pick[...].astype(BF), NT, preferred_element_type=F32)
    hit = jnp.zeros((PL, TOK), F32)
    for k in range(TOP):
        route = routes_t[k : k + 1, :]
        p = pick_t[k : k + 1, :]
        by2 = p - jnp.where(p >= 2.0, 2.0, 0.0) - jnp.where(p >= 4.0, 2.0, 0.0)
        by3 = p - jnp.where(p >= 3.0, 3.0, 0.0)
        wanted = jnp.where(copies == 1.0, 0.0, jnp.where(copies == 2.0, by2, by3))
        hit = hit + jnp.where((route == plc_col) & (wanted == order), 1.0, 0.0)
    names = (plc_col == lax.broadcasted_iota(jnp.int32, (PL, EXPERTS), 1).astype(F32)).astype(BF)
    router_rows = lax.dot_general(names, router[...], NT, preferred_element_type=F32).astype(BF)

    for r in orings:
        r.arrive(3)
    for r in orings:
        r.from_partner()

    for q in range(4):
        cols = pl.ds(q * QW, QW)
        projected = jnp.dot(ho_v[...], wo[q], preferred_element_type=F32)
        hid[:, cols] = (res_v[:, cols].astype(F32) + projected).astype(BF)
    normed = rms(hid[...].astype(F32), ngain[...]).astype(BF)
    logits = lax.dot_general(router_rows, normed, NT, preferred_element_type=F32)
    raised = jnp.where(hit > 0.0, jnp.exp(logits), 0.0)
    weight = (raised / jnp.sum(raised, axis=0, keepdims=True)).astype(BF)
    for q in range(4):
        xq[q, chip, 0:TOK, :] = normed[:, q * QW : (q + 1) * QW]
    xq[0, chip, TOK : TOK + 32, 0:128] = weight[0:32, :]
    xq[0, chip, TOK : TOK + 32, 128:256] = weight[32:64, :]

    def axes(q):
        return (x, y, xnb, ynb) if q < 2 else (y, x, ynb, xnb)

    def cid(q, aa, bb):
        return aa * NY + bb if q < 2 else bb * NY + aa

    def block(q, idx):
        return xq.at[q, idx, pl.ds(0, TOK + 32 if q == 0 else TOK), :]

    def back(v, dirn, k):
        return wrap(v - k, 4) if dirn == 0 else wrap(v + k, 4)

    def hop_index(q, dirn, k):
        return k if dirn == 0 else PHOPS[q % 2][0] + k

    def a1_go(q, dirn, k):
        a, b, na, nb = axes(q)
        at = block(q, cid(q, back(a, dirn, k), b))
        i = hop_index(q, dirn, k)
        send(at, at, a1_s.at[q, i], a1_r.at[q, i], na[dirn])

    def a2_go(q, label, aa, dirn, k):
        a, b, na, nb = axes(q)
        at = block(q, cid(q, aa, back(b, dirn, k)))
        i = hop_index(q, dirn, k)
        send(at, at, a2_s.at[q, label, i], a2_r.at[q, label, i], nb[dirn])

    def a1_arrive(q, dirn, k):
        a, b, na, nb = axes(q)
        aa = back(a, dirn, k + 1)
        i = hop_index(q, dirn, k)
        arrived(block(q, cid(q, aa, b)), a1_s.at[q, i], a1_r.at[q, i])
        if k + 1 < PHOPS[q % 2][dirn]:
            a1_go(q, dirn, k + 1)
        for d2 in range(2):
            a2_go(q, 1 + i, aa, d2, 0)

    def a2_arrive(q, label, aa, dirn, k):
        a, b, na, nb = axes(q)
        i = hop_index(q, dirn, k)
        arrived(block(q, cid(q, aa, back(b, dirn, k + 1))), a2_s.at[q, label, i], a2_r.at[q, label, i])
        if k + 1 < PHOPS[q % 2][dirn]:
            a2_go(q, label, aa, dirn, k + 1)

    for q in range(4):
        a = axes(q)[0]
        for dirn in range(2):
            a1_go(q, dirn, 0)
        for dirn in range(2):
            a2_go(q, 0, a, dirn, 0)
    events = []
    for q in range(4):
        a = axes(q)[0]
        hops = [(dirn, k) for dirn in range(2) for k in range(PHOPS[q % 2][dirn])]
        for d2, k2 in hops:
            events.append((k2 + 1, q, functools.partial(a2_arrive, q, 0, a, d2, k2)))
        for dirn, k in hops:
            events.append((k + 1, q, functools.partial(a1_arrive, q, dirn, k)))
            aa = back(a, dirn, k + 1)
            label = 1 + hop_index(q, dirn, k)
            for d2, k2 in hops:
                events.append((k + k2 + 2, q, functools.partial(a2_arrive, q, label, aa, d2, k2)))
    events.sort(key=lambda ev: ev[:2])
    for n, (_, _, run) in enumerate(events):
        run()
        if n % 15 == 14:
            pump()

    lane32 = lax.broadcasted_iota(jnp.int32, (TOP, 32), 1)
    row32 = lax.broadcasted_iota(jnp.int32, (TOP, 32), 0)
    mine = SLOTS * chip + row32
    pick_lo = ((lane32 == mine) & (row32 < SLOTS)).astype(BF)
    pick_hi = ((lane32 + 32 == mine) & (row32 < SLOTS)).astype(BF)

    def take_weights(s, carry):
        table = xq[0, s, TOK : TOK + 32, :]
        wt[pl.ds(pl.multiple_of(s * 8, 8), 8), :] = jnp.dot(
            pick_lo, table[:, 0:128], preferred_element_type=F32
        ) + jnp.dot(pick_hi, table[:, 128:256], preferred_element_type=F32)
        return carry

    lax.fori_loop(0, CHIPS, take_weights, 0)
    weights = wt[0:128, :]
    rows128 = lax.broadcasted_iota(jnp.int32, (TOK, TOK), 0)
    cols128 = lax.broadcasted_iota(jnp.int32, (TOK, TOK), 1)
    earlier = (rows128 < cols128).astype(BF)
    taken = weights > 0.0
    rank = jnp.dot(taken.astype(BF), earlier, preferred_element_type=F32)
    wt[pl.ds(128, 128), :] = jnp.where(taken, rank, -1.0)

    def compact(s, carry):
        base = pl.multiple_of(s * 8, 8)
        w8 = wt[pl.ds(base, 8), :]
        r8 = wt[pl.ds(pl.multiple_of(128 + s * 8, 8), 8), :]
        rows = lax.broadcasted_iota(jnp.int32, (CAP, TOK), 0).astype(F32)
        here = [rows == r8[j : j + 1, :] for j in range(SLOTS)]
        chosen = jnp.concatenate([jnp.where(h, 1.0, 0.0) for h in here], axis=0).astype(BF)
        pw[s] = jnp.concatenate(
            [jnp.where(here[j], w8[j : j + 1, :], 0.0) for j in range(SLOTS)], axis=0
        ).astype(BF)
        tokens = jnp.concatenate([xq[q, s, 0:TOK, :] for q in range(4)], axis=1)
        packed = jnp.dot(chosen, tokens, preferred_element_type=F32).astype(BF)
        for j in range(SLOTS):
            xc[j, pl.ds(pl.multiple_of(s * CAP, 16), CAP), :] = packed[j * CAP : (j + 1) * CAP, :]
        return carry

    for g in range(2):
        lax.fori_loop(g * 8, g * 8 + 8, compact, 0)
        pump()

    def gate_up(c, n, carry):
        j = lax.div(n, 3)
        at = pl.ds(pl.multiple_of(lax.rem(n, 3) * 256, 256), 256)
        both = jnp.dot(xc[j, at, :], wgu[c, j], preferred_element_type=F32)
        g, u = both[:, 0:HALF], both[:, HALF:]
        act[j, at, c * HALF : (c + 1) * HALF] = (g / (1.0 + jnp.exp(-g)) * u).astype(BF)
        return carry

    while len(zqueue) > 4:
        pump()
    for r in pieces[0]:
        r.from_partner()
    for g in range(2):
        lax.fori_loop(g * 6, g * 6 + 6, functools.partial(gate_up, 0), 0)
        pump()
    while zqueue:
        pump()
    for r in pieces[1] + pieces[2]:
        r.from_partner()
    lax.fori_loop(0, 12, functools.partial(gate_up, 1), 0)

    def down(n, carry):
        j = lax.div(n, 3)
        at = pl.ds(pl.multiple_of(lax.rem(n, 3) * 256, 256), 256)
        yc[j, at, :] = jnp.dot(act[j, at, :], wd[j], preferred_element_type=F32).astype(BF)
        return carry

    lax.fori_loop(0, 12, down, 0)

    def combine(s, carry):
        at = pl.ds(pl.multiple_of(s * CAP, 16), CAP)
        outs = jnp.concatenate([yc[j, at, :] for j in range(SLOTS)], axis=0)
        total = lax.dot_general(pw[s], outs, TN, preferred_element_type=F32).astype(BF)
        for q in range(4):
            part[q, s] = total[:, q * QW : (q + 1) * QW]
        return carry

    lax.fori_loop(0, CHIPS, combine, 0)

    def ahead(v, h, dirn, k):
        left = h - k
        return wrap(v + left, 4) if dirn == 0 else wrap(v - left, 4)

    def s1_go(q, o, dirn, k):
        a, b, na, nb = axes(q)
        i = hop_index(q, dirn, k)
        target = cid(q, ahead(a, PHOPS[q % 2][dirn], dirn, k), wrap(b + o, 4))
        send(part.at[q, target], rb1.at[q, i, o], r1_s.at[q, i, o], r1_r.at[q, i, o], na[dirn])

    def s2_go(q, dirn, k):
        a, b, na, nb = axes(q)
        i = hop_index(q, dirn, k)
        target = cid(q, a, ahead(b, PHOPS[q % 2][dirn], dirn, k))
        send(part.at[q, target], rb2.at[q, i], r2_s.at[q, i], r2_r.at[q, i], nb[dirn])

    def s1_wait(q, o, dirn, k):
        i = hop_index(q, dirn, k)
        arrived(rb1.at[q, i, o], r1_s.at[q, i, o], r1_r.at[q, i, o])
        return rb1[q, i, o].astype(F32)

    def s2_wait(q, dirn, k):
        i = hop_index(q, dirn, k)
        arrived(rb2.at[q, i], r2_s.at[q, i], r2_r.at[q, i])
        return rb2[q, i].astype(F32)

    def add_into(q, idx, *terms):
        total = part[q, idx].astype(F32)
        for t in terms:
            total = total + t
        part[q, idx] = total.astype(BF)

    offsets = (2, 1, 3, 0)
    for o in offsets:
        for q in range(4):
            for dirn in range(2):
                s1_go(q, o, dirn, 0)
    for o in offsets:
        for q in range(4):
            a, b, na, nb = axes(q)
            far = 0 if PHOPS[q % 2][0] == 2 else 1
            add_into(q, cid(q, ahead(a, 2, far, 1), wrap(b + o, 4)), s1_wait(q, o, far, 0))
            s1_go(q, o, far, 1)
    own = [None] * 4
    for o in offsets:
        for q in range(4):
            a, b, na, nb = axes(q)
            right, left = PHOPS[q % 2]
            terms = [s1_wait(q, o, 0, right - 1), s1_wait(q, o, 1, left - 1)]
            far = 0 if right == 2 else 1
            mid = 1 if far == 0 else 3
            add_into(q, cid(q, a, wrap(b + o, 4)), *terms)
            if o == 2:
                s2_go(q, far, 0)
            elif o == 4 - mid:
                s2_go(q, 1 - far, 0)
    for q in range(4):
        a, b, na, nb = axes(q)
        far = 0 if PHOPS[q % 2][0] == 2 else 1
        add_into(q, cid(q, a, ahead(b, 2, far, 1)), s2_wait(q, far, 0))
        s2_go(q, far, 1)
    for q in range(4):
        right, left = PHOPS[q % 2]
        own[q] = part[q, chip].astype(F32) + s2_wait(q, 0, right - 1) + s2_wait(q, 1, left - 1)
    mixture = jnp.concatenate(own, axis=1)
    out_ref[...] = rms(hid[...].astype(F32) + mixture, fgain[...]).astype(BF)

    for copy in sends:
        copy.wait_send()


def body(
    head_outputs,
    residual,
    output_weight,
    router,
    norm_gain,
    placed_gate_up,
    placed_down,
    routes,
    replica_pick,
    placement,
    final_gain,
):
    dma = pltpu.SemaphoreType.DMA
    anywhere = pl.BlockSpec(memory_space=pl.ANY)
    vmem = pl.BlockSpec(memory_space=pltpu.VMEM)
    return pl.pallas_call(
        body_kernel,
        out_shape=jax.ShapeDtypeStruct((TOK, D), BF),
        in_specs=[anywhere] * 5 + [vmem] * 6,
        out_specs=vmem,
        scratch_shapes=[
            pltpu.VMEM((TOK, D), BF),
            pltpu.VMEM((TOK, D), BF),
            pltpu.VMEM((4, D, QW), BF),
            pltpu.VMEM((2, SLOTS, D, FF), BF),
            pltpu.VMEM((SLOTS, FF, D), BF),
            pltpu.VMEM((4, CHIPS, TOK + 32, QW), BF),
            pltpu.VMEM((SLOTS, ROWS, D), BF),
            pltpu.VMEM((SLOTS, ROWS, FF), BF),
            pltpu.VMEM((SLOTS, ROWS, D), BF),
            pltpu.VMEM((4, CHIPS, TOK, QW), BF),
            pltpu.VMEM((4, 3, 4, TOK, QW), BF),
            pltpu.VMEM((4, 3, TOK, QW), BF),
            pltpu.VMEM((TOK, D), BF),
            pltpu.VMEM((256, TOK), F32),
            pltpu.VMEM((CHIPS, SLOTS * CAP, TOK), BF),
            dma((16,)),
            dma((2, 8)),
            dma((2, 8)),
            dma((2, 8)),
            dma((2, 8)),
            dma((6, 8)),
            dma((6, 8)),
            dma((6, 9)),
            dma((6, 9)),
            dma((4, 3)),
            dma((4, 3)),
            dma((4, 4, 3)),
            dma((4, 4, 3)),
            dma((4, 3, 4)),
            dma((4, 3, 4)),
            dma((4, 3)),
            dma((4, 3)),
        ],
        compiler_params=pltpu.CompilerParams(
            collective_id=0, has_side_effects=True, vmem_limit_bytes=60 * 1024 * 1024
        ),
    )(
        head_outputs,
        residual,
        output_weight,
        placed_gate_up,
        placed_down,
        router,
        norm_gain.reshape(1, D),
        final_gain.reshape(1, D),
        routes,
        replica_pick,
        placement.reshape(1, PL),
    )


def solution(mesh):
    return jax.shard_map(
        body,
        mesh=mesh,
        in_specs=(
            P(("expert", "shard"), None),
            P(("expert", "shard"), None),
            P("shard", None),
            P(),
            P(),
            P("expert", "shard", None),
            P("expert", "shard", None),
            P(("expert", "shard"), None),
            P(("expert", "shard"), None),
            P(),
            P(),
        ),
        out_specs=P(("expert", "shard"), None),
        check_vma=False,
    )
```

time: 299 us -> 144 us (0.48)
  waiting for transfers between devices: 199 us -> 0 us
  Pallas kernels: 0 us -> 137 us
  matrix products: 24.8 us -> 0 us
  other arithmetic: 24.1 us -> 0 us
  local copies, waits for them, and re-layouts: 23.9 us -> 4.66 us
  starting transfers between devices: 13.4 us -> 0 us
  between operations: 13.3 us -> 0.01 us
    pallas_call x0 -> x1, Pallas kernels: none -> 137 us  [body(): pl.pallas_call(body_kernel, out_shape=jax.ShapeDtypeStruct((TOK, D), BF),...]
    all_gather x3 -> x0, waiting for transfers between devices: 99.3 us -> none  [the longest x1 55 us: body(): lax.all_gather(placed_gate_up, 'shard', axis=1, tiled=True)]
    all_to_all x2 -> x0, waiting for transfers between devices: 97.8 us -> none  [the longest x1 87.8 us: body(): lax.all_to_all(answers.reshape(groups, slot_count * capacity, model_width...]
    dot_general x10 -> x0, matrix products: 24.8 us -> none  [the longest x4 18.4 us: apply_block(): jnp.einsum('bjmd,jdf->bjmf', block_part, gate_up, preferred_element_type=...]
    another operation x4 -> x0, other arithmetic: 18.4 us -> none
    all_to_all x2 -> x0, starting transfers between devices: 13.3 us -> none  [the longest x1 8.19 us: body(): lax.all_to_all(outbound.reshape(groups, slot_count * capacity, model_widt...]
    scatter x1 -> x0, local copies, waits for them, and re-layouts: 9.04 us -> none  [body(): outbound = jnp.zeros((place_count * capacity, model_width), jnp.bfloat16)...]
    gather x1 -> x0, local copies, waits for them, and re-layouts: 8.57 us -> none  [body(): returned[buffer_index].reshape(row_count, route_count, model_width)]
  transfers between devices with their start and end apart: 5 -> 0, of which waited for: 5 -> 0; matrix products, arithmetic and copies ran while one was open for 11% -> 0% of each run, Pallas kernels for 0% -> 0%
where the time goes in v1:
time: 144 us; the launch traced here: 142 us
  Pallas kernels  137 us (95%)
  local copies, waits for them, and re-layouts  4.66 us (3%)
    pallas_call x1, Pallas kernels, body(): pl.pallas_call(body_kernel, out_shape=jax.ShapeDtypeStruct((TOK, D), BF),...  137 us
    unnamed x10, local copies, waits for them, and re-layouts  4.66 us

profile of v1, /device:TPU:8, one launch (start us, length us, event | category | flops | bytes accessed | tf_op | source)
XLA Modules:
  0.0 142.1 jit_solution(4819650072641832794)
XLA Ops:
  0.0 0.0 copy-start.1
  0.0 0.7 copy-done.1
  0.7 0.0 copy-start.2
  0.7 0.0 copy-start
  0.7 0.7 copy.13.routes
  1.4 0.0 copy-done.2
  1.4 0.7 copy.14.pick
  2.2 0.0 copy-done
  2.2 0.8 copy.12.router
  3.0 137.5 %shard_map.109 = bf16[128,1024]{1,0:T(8,128)(2,1)} custom-call(bf16[128,1024]{1,0:T(8,128)(2,1)} %ho.1, bf16[128,1024]{1,0:T(8,128)(2,1)} %res.1, bf16[128,1024]{1,0:T(8,128)(2,1)} %wo_in.1, bf16[2,128,1024]{2,1,0:T(8,128)(2,1)} %gu_in.1, bf16[2,64,1024]{2,1,0:T(8,128)(2,1)} %dn_in.1, bf16[1024,32]{1,0:T(8,128)(2,1)} %copy.12.router, f32[1,1024]{1,0:T(1,128)} %bitcast.3, ...), custom_call_target="tpu_custom_call" | custom-call | tf_op jit(solution)/shard_map/pallas_call | solution.py:521
  140.5 1.7 %copy.16 = bf16[128,1024]{1,0:T(8,128)(2,1)} copy(bf16[128,1024]{1,0:T(8,128)(2,1)} %shard_map.109) | data formatting | bytes 524288
Async XLA Ops:
  0.0 0.7 copy-start.1
  0.7 0.7 copy-start.2
  0.7 1.5 %copy-start = (bf16[1024,32]{0,1:T(8,128)(2,1)S(1)}, bf16[1024,32]{0,1:T(8,128)(2,1)}, u32[]{:S(2)}) copy-start(bf16[1024,32]{0,1:T(8,128)(2,1)} %param.14) | copy-start | bytes 196612

commit v2 on v1

--- a/solution.py
+++ b/solution.py
@@ -17,6 +17,7 @@
 CAP = 48
 PL = 64
 QW = 256
+HW = 512
 HALF = FF // 2
 SLOTS = 4
 ROWS = CHIPS * CAP
@@ -25,7 +26,7 @@
 BF = jnp.bfloat16
 F32 = jnp.float32
 ZHOPS = ((4, 3), (3, 4))
-PHOPS = ((2, 1), (1, 2))
+PHOPS = ((2, 1), (1, 2), (1, 2), (2, 1))
 NT = (((1,), (1,)), ((), ()))
 TN = (((0,), (0,)), ((), ()))
 
@@ -132,8 +133,9 @@
             s = 2 * core + j
             load(gu_in.at[j, :, pl.ds(c * HALF, HALF)], wgu.at[c, s, zrow, pl.ds(0, HALF)])
             load(gu_in.at[j, :, pl.ds(FF + c * HALF, HALF)], wgu.at[c, s, zrow, pl.ds(HALF, HALF)])
-    for j in range(2):
-        load(dn_in.at[j], wd.at[2 * core + j, zrow2, :])
+    for h in range(2):
+        for j in range(2):
+            load(dn_in.at[j, :, pl.ds(h * HW, HW)], wd.at[h, 2 * core + j, zrow2, :])
 
     barrier = pltpu.get_barrier_semaphore()
     for nb in (partner,) + znb + xnb + ynb:
@@ -189,8 +191,8 @@
     def gu_at(c, j):
         return lambda cc, zz: wgu.at[c, 2 * cc + j, pl.ds(pl.multiple_of(zz * 128, 128), 128), :]
 
-    def dn_at(j):
-        return lambda cc, zz: wd.at[2 * cc + j, pl.ds(pl.multiple_of(zz * 64, 64), 64), :]
+    def dn_at(h, j):
+        return lambda cc, zz: wd.at[h, 2 * cc + j, pl.ds(pl.multiple_of(zz * 64, 64), 64), :]
 
     def sem_row(ref, u):
         return lambda i: ref.at[u, i]
@@ -200,46 +202,43 @@
 
     orings = [ring(wo_at(i), i, ZHOPS[i], (o_s, o_r, op_s, op_r), False) for i in range(2)]
     zrefs = (z_s, z_r, zp_s, zp_r)
-    pieces = [
-        [ring(gu_at(0, j), j, ZHOPS[j], zrefs, True) for j in range(2)],
-        [ring(dn_at(j), 2 + j, ZHOPS[j], zrefs, True) for j in range(2)],
-        [ring(gu_at(1, j), 4 + j, ZHOPS[j], zrefs, True) for j in range(2)],
+    gu = [[ring(gu_at(c, j), 2 * c + j, ZHOPS[j], zrefs, True) for j in range(2)] for c in range(2)]
+    dn = [[ring(dn_at(h, j), 4 + 2 * h + j, ZHOPS[j], zrefs, True) for j in range(2)] for h in range(2)]
+
+    zqueue = [
+        (21, gu[0], 0),
+        (27, gu[1], 0),
+        (32, gu[0], 1),
+        (38, gu[1], 1),
+        (44, gu[0], 2),
+        (45, dn[0], 0),
+        (49, gu[1], 2),
+        (52, dn[0], 1),
+        (53, dn[1], 0),
+        (54, gu[0], 3),
+        (57, dn[0], 2),
+        (58, gu[1], 3),
+        (60, dn[1], 1),
+        (62, dn[0], 3),
+        (64, dn[1], 2),
+        (68, dn[1], 3),
     ]
 
-    def z_begin(p):
-        for r in pieces[p]:
-            r.begin()
-
-    def z_arrive(p, k):
-        for r in pieces[p]:
-            r.arrive(k)
-
-    zqueue = [
-        lambda: z_arrive(0, 0),
-        lambda: z_arrive(1, 0),
-        lambda: (z_arrive(0, 1), z_begin(2)),
-        lambda: z_arrive(1, 1),
-        lambda: z_arrive(0, 2),
-        lambda: z_arrive(2, 0),
-        lambda: z_arrive(1, 2),
-        lambda: z_arrive(0, 3),
-        lambda: z_arrive(2, 1),
-        lambda: z_arrive(1, 3),
-        lambda: z_arrive(2, 2),
-        lambda: z_arrive(2, 3),
-    ]
-
-    def pump():
-        if zqueue:
-            zqueue.pop(0)()
+    def pump(now):
+        while zqueue and zqueue[0][0] <= now:
+            _, rings, k = zqueue.pop(0)
+            for r in rings:
+                r.arrive(k)
 
     for r in orings:
         r.begin()
+    dn[0][0].begin()
     for k in range(3):
         for r in orings:
             r.arrive(k)
-    z_begin(0)
-    z_begin(1)
+        (dn[0][1], dn[1][0], dn[1][1])[k].begin()
+    for r in gu[0] + gu[1]:
+        r.begin()
 
     plc_row = plc[...].astype(F32)
     rows64 = lax.broadcasted_iota(jnp.int32, (PL, PL), 0)
@@ -283,10 +282,10 @@
     xq[0, chip, TOK : TOK + 32, 128:256] = weight[32:64, :]
 
     def axes(q):
-        return (x, y, xnb, ynb) if q < 2 else (y, x, ynb, xnb)
+        return (x, y, xnb, ynb) if q % 2 == 0 else (y, x, ynb, xnb)
 
     def cid(q, aa, bb):
-        return aa * NY + bb if q < 2 else bb * NY + aa
+        return aa * NY + bb if q % 2 == 0 else bb * NY + aa
 
     def block(q, idx):
         return xq.at[q, idx, pl.ds(0, TOK + 32 if q == 0 else TOK), :]
@@ -295,7 +294,7 @@
         return wrap(v - k, 4) if dirn == 0 else wrap(v + k, 4)
 
     def hop_index(q, dirn, k):
-        return k if dirn == 0 else PHOPS[q % 2][0] + k
+        return k if dirn == 0 else PHOPS[q][0] + k
 
     def a1_go(q, dirn, k):
         a, b, na, nb = axes(q)
@@ -314,7 +313,7 @@
         aa = back(a, dirn, k + 1)
         i = hop_index(q, dirn, k)
         arrived(block(q, cid(q, aa, b)), a1_s.at[q, i], a1_r.at[q, i])
-        if k + 1 < PHOPS[q % 2][dirn]:
+        if k + 1 < PHOPS[q][dirn]:
             a1_go(q, dirn, k + 1)
         for d2 in range(2):
             a2_go(q, 1 + i, aa, d2, 0)
@@ -323,7 +322,7 @@
         a, b, na, nb = axes(q)
         i = hop_index(q, dirn, k)
         arrived(block(q, cid(q, aa, back(b, dirn, k + 1))), a2_s.at[q, label, i], a2_r.at[q, label, i])
-        if k + 1 < PHOPS[q % 2][dirn]:
+        if k + 1 < PHOPS[q][dirn]:
             a2_go(q, label, aa, dirn, k + 1)
 
     for q in range(4):
@@ -335,7 +334,7 @@
     events = []
     for q in range(4):
         a = axes(q)[0]
-        hops = [(dirn, k) for dirn in range(2) for k in range(PHOPS[q % 2][dirn])]
+        hops = [(dirn, k) for dirn in range(2) for k in range(PHOPS[q][dirn])]
         for d2, k2 in hops:
             events.append((k2 + 1, q, functools.partial(a2_arrive, q, 0, a, d2, k2)))
         for dirn, k in hops:
@@ -346,9 +345,8 @@
                 events.append((k + k2 + 2, q, functools.partial(a2_arrive, q, label, aa, d2, k2)))
     events.sort(key=lambda ev: ev[:2])
     for n, (_, _, run) in enumerate(events):
+        pump(22.5 + 0.42 * n)
         run()
-        if n % 15 == 14:
-            pump()
 
     lane32 = lax.broadcasted_iota(jnp.int32, (TOP, 32), 1)
     row32 = lax.broadcasted_iota(jnp.int32, (TOP, 32), 0)
@@ -388,9 +386,9 @@
             xc[j, pl.ds(pl.multiple_of(s * CAP, 16), CAP), :] = packed[j * CAP : (j + 1) * CAP, :]
         return carry
 
-    for g in range(2):
-        lax.fori_loop(g * 8, g * 8 + 8, compact, 0)
-        pump()
+    for g in range(4):
+        lax.fori_loop(g * 4, g * 4 + 4, compact, 0)
+        pump((45, 46, 50, 53)[g])
 
     def gate_up(c, n, carry):
         j = lax.div(n, 3)
@@ -400,36 +398,32 @@
         act[j, at, c * HALF : (c + 1) * HALF] = (g / (1.0 + jnp.exp(-g)) * u).astype(BF)
         return carry
 
-    while len(zqueue) > 4:
-        pump()
-    for r in pieces[0]:
+    pump(54)
+    for r in gu[0]:
         r.from_partner()
     for g in range(2):
         lax.fori_loop(g * 6, g * 6 + 6, functools.partial(gate_up, 0), 0)
-        pump()
-    while zqueue:
-        pump()
-    for r in pieces[1] + pieces[2]:
+        pump((57, 60)[g])
+    for r in gu[1]:
         r.from_partner()
-    lax.fori_loop(0, 12, functools.partial(gate_up, 1), 0)
-
-    def down(n, carry):
+    for g in range(2):
+        lax.fori_loop(g * 6, g * 6 + 6, functools.partial(gate_up, 1), 0)
+        pump((62, 64)[g])
+
+    def down(h, n, carry):
         j = lax.div(n, 3)
         at = pl.ds(pl.multiple_of(lax.rem(n, 3) * 256, 256), 256)
-        yc[j, at, :] = jnp.dot(act[j, at, :], wd[j], preferred_element_type=F32).astype(BF)
+        out = jnp.dot(act[j, at, :], wd[h, j], preferred_element_type=F32)
+        yc[j, at, h * HW : (h + 1) * HW] = out.astype(BF)
         return carry
 
-    lax.fori_loop(0, 12, down, 0)
-
-    def combine(s, carry):
+    def combine(h, s, carry):
         at = pl.ds(pl.multiple_of(s * CAP, 16), CAP)
-        outs = jnp.concatenate([yc[j, at, :] for j in range(SLOTS)], axis=0)
+        outs = jnp.concatenate([yc[j, at, h * HW : (h + 1) * HW] for j in range(SLOTS)], axis=0)
         total = lax.dot_general(pw[s], outs, TN, preferred_element_type=F32).astype(BF)
-        for q in range(4):
-            part[q, s] = total[:, q * QW : (q + 1) * QW]
+        for i in range(2):
+            part[2 * h + i, s] = total[:, i * QW : (i + 1) * QW]
         return carry
-
-    lax.fori_loop(0, CHIPS, combine, 0)
 
     def ahead(v, h, dirn, k):
         left = h - k
@@ -438,13 +432,13 @@
     def s1_go(q, o, dirn, k):
         a, b, na, nb = axes(q)
         i = hop_index(q, dirn, k)
-        target = cid(q, ahead(a, PHOPS[q % 2][dirn], dirn, k), wrap(b + o, 4))
+        target = cid(q, ahead(a, PHOPS[q][dirn], dirn, k), wrap(b + o, 4))
         send(part.at[q, target], rb1.at[q, i, o], r1_s.at[q, i, o], r1_r.at[q, i, o], na[dirn])
 
     def s2_go(q, dirn, k):
         a, b, na, nb = axes(q)
         i = hop_index(q, dirn, k)
-        target = cid(q, a, ahead(b, PHOPS[q % 2][dirn], dirn, k))
+        target = cid(q, a, ahead(b, PHOPS[q][dirn], dirn, k))
         send(part.at[q, target], rb2.at[q, i], r2_s.at[q, i], r2_r.at[q, i], nb[dirn])
 
     def s1_wait(q, o, dirn, k):
@@ -464,37 +458,66 @@
         part[q, idx] = total.astype(BF)
 
     offsets = (2, 1, 3, 0)
-    for o in offsets:
-        for q in range(4):
-            for dirn in range(2):
-                s1_go(q, o, dirn, 0)
-    for o in offsets:
-        for q in range(4):
+    own = [None] * 4
+
+    def s1_first(h):
+        for o in offsets:
+            for q in (2 * h, 2 * h + 1):
+                for dirn in range(2):
+                    s1_go(q, o, dirn, 0)
+
+    def s1_far(h):
+        for o in offsets:
+            for q in (2 * h, 2 * h + 1):
+                a, b, na, nb = axes(q)
+                far = 0 if PHOPS[q][0] == 2 else 1
+                add_into(q, cid(q, ahead(a, 2, far, 1), wrap(b + o, 4)), s1_wait(q, o, far, 0))
+                s1_go(q, o, far, 1)
+
+    def s1_end(h):
+        for o in offsets:
+            for q in (2 * h, 2 * h + 1):
+                a, b, na, nb = axes(q)
+                right, left = PHOPS[q]
+                terms = [s1_wait(q, o, 0, right - 1), s1_wait(q, o, 1, left - 1)]
+                far = 0 if right == 2 else 1
+                mid = 1 if far == 0 else 3
+                add_into(q, cid(q, a, wrap(b + o, 4)), *terms)
+                if o == 2:
+                    s2_go(q, far, 0)
+                elif o == 4 - mid:
+                    s2_go(q, 1 - far, 0)
+
+    def s2_far(h):
+        for q in (2 * h, 2 * h + 1):
             a, b, na, nb = axes(q)
-            far = 0 if PHOPS[q % 2][0] == 2 else 1
-            add_into(q, cid(q, ahead(a, 2, far, 1), wrap(b + o, 4)), s1_wait(q, o, far, 0))
-            s1_go(q, o, far, 1)
-    own = [None] * 4
-    for o in offsets:
-        for q in range(4):
-            a, b, na, nb = axes(q)
-            right, left = PHOPS[q % 2]
-            terms = [s1_wait(q, o, 0, right - 1), s1_wait(q, o, 1, left - 1)]
-            far = 0 if right == 2 else 1
-            mid = 1 if far == 0 else 3
-            add_into(q, cid(q, a, wrap(b + o, 4)), *terms)
-            if o == 2:
-                s2_go(q, far, 0)
-            elif o == 4 - mid:
-                s2_go(q, 1 - far, 0)
-    for q in range(4):
-        a, b, na, nb = axes(q)
-        far = 0 if PHOPS[q % 2][0] == 2 else 1
-        add_into(q, cid(q, a, ahead(b, 2, far, 1)), s2_wait(q, far, 0))
-        s2_go(q, far, 1)
-    for q in range(4):
-        right, left = PHOPS[q % 2]
-        own[q] = part[q, chip].astype(F32) + s2_wait(q, 0, right - 1) + s2_wait(q, 1, left - 1)
+            far = 0 if PHOPS[q][0] == 2 else 1
+            add_into(q, cid(q, a, ahead(b, 2, far, 1)), s2_wait(q, far, 0))
+            s2_go(q, far, 1)
+
+    def s2_end(h):
+        for q in (2 * h, 2 * h + 1):
+            right, left = PHOPS[q]
+            own[q] = part[q, chip].astype(F32) + s2_wait(q, 0, right - 1) + s2_wait(q, 1, left - 1)
+
+    def produce(h):
+        for r in dn[h]:
+            r.from_partner()
+        lax.fori_loop(0, 12, functools.partial(down, h), 0)
+        lax.fori_loop(0, CHIPS, functools.partial(combine, h), 0)
+        s1_first(h)
+        pump(68)
+
+    produce(0)
+    produce(1)
+    s1_far(0)
+    s1_far(1)
+    s1_end(0)
+    s2_far(0)
+    s1_end(1)
+    s2_far(1)
+    s2_end(0)
+    s2_end(1)
     mixture = jnp.concatenate(own, axis=1)
     out_ref[...] = rms(hid[...].astype(F32) + mixture, fgain[...]).astype(BF)
 
@@ -528,7 +551,7 @@
             pltpu.VMEM((TOK, D), BF),
             pltpu.VMEM((4, D, QW), BF),
             pltpu.VMEM((2, SLOTS, D, FF), BF),
-            pltpu.VMEM((SLOTS, FF, D), BF),
+            pltpu.VMEM((2, SLOTS, FF, HW), BF),
             pltpu.VMEM((4, CHIPS, TOK + 32, QW), BF),
             pltpu.VMEM((SLOTS, ROWS, D), BF),
             pltpu.VMEM((SLOTS, ROWS, FF), BF),
@@ -539,15 +562,15 @@
             pltpu.VMEM((TOK, D), BF),
             pltpu.VMEM((256, TOK), F32),
             pltpu.VMEM((CHIPS, SLOTS * CAP, TOK), BF),
-            dma((16,)),
+            dma((18,)),
             dma((2, 8)),
             dma((2, 8)),
             dma((2, 8)),
             dma((2, 8)),
-            dma((6, 8)),
-            dma((6, 8)),
-            dma((6, 9)),
-            dma((6, 9)),
+            dma((8, 8)),
+            dma((8, 8)),
+            dma((8, 9)),
+            dma((8, 9)),
             dma((4, 3)),
             dma((4, 3)),
             dma((4, 4, 3)),

time: 144 us -> 131 us (0.910); the launches traced: 142 us -> 131 us
  Pallas kernels: 137 us -> 126 us
    pallas_call x1, Pallas kernels: 137 us -> 126 us  [body(): pl.pallas_call(body_kernel, out_shape=jax.ShapeDtypeStruct((TOK, D), BF),...]
where the time goes in v2:
time: 131 us
  Pallas kernels  126 us (96%)
  local copies, waits for them, and re-layouts  4.66 us (4%)
    pallas_call x1, Pallas kernels, body(): pl.pallas_call(body_kernel, out_shape=jax.ShapeDtypeStruct((TOK, D), BF),...  126 us
    unnamed x10, local copies, waits for them, and re-layouts  4.66 us

profile of v2, /device:TPU:8, one launch (start us, length us, event | category | flops | bytes accessed | tf_op | source)
XLA Modules:
  0.0 130.8 jit_solution(642635430982208299)
XLA Ops:
  0.0 0.0 copy-start.1
  0.0 0.7 copy-done.1
  0.7 0.0 copy-start.2
  0.7 0.0 copy-start
  0.7 0.7 copy.13.routes
  1.4 0.0 copy-done.2
  1.4 0.7 copy.14.pick
  2.2 0.0 copy-done
  2.2 0.8 copy.12.router
  3.0 126.2 %shard_map.109 = bf16[128,1024]{1,0:T(8,128)(2,1)} custom-call(bf16[128,1024]{1,0:T(8,128)(2,1)} %ho.1, bf16[128,1024]{1,0:T(8,128)(2,1)} %res.1, bf16[128,1024]{1,0:T(8,128)(2,1)} %wo_in.1, bf16[2,128,1024]{2,1,0:T(8,128)(2,1)} %gu_in.1, bf16[2,64,1024]{2,1,0:T(8,128)(2,1)} %dn_in.1, bf16[1024,32]{1,0:T(8,128)(2,1)} %copy.12.router, f32[1,1024]{1,0:T(1,128)} %bitcast.3, ...), custom_call_target="tpu_custom_call" | custom-call | tf_op jit(solution)/shard_map/pallas_call | solution.py:544
  129.2 1.7 %copy.16 = bf16[128,1024]{1,0:T(8,128)(2,1)} copy(bf16[128,1024]{1,0:T(8,128)(2,1)} %shard_map.109) | data formatting | bytes 524288
Async XLA Ops:
  0.0 0.7 copy-start.1
  0.7 0.7 copy-start.2
  0.7 1.5 %copy-start = (bf16[1024,32]{0,1:T(8,128)(2,1)S(1)}, bf16[1024,32]{0,1:T(8,128)(2,1)}, u32[]{:S(2)}) copy-start(bf16[1024,32]{0,1:T(8,128)(2,1)} %param.14) | copy-start | bytes 196612

commit v3 on v2

--- a/solution.py
+++ b/solution.py
@@ -66,7 +66,6 @@
     rb1,
     rb2,
     hid,
-    wt,
     pw,
     lsem,
     o_r,
@@ -247,11 +246,8 @@
     same = plc_col == plc_row
     copies = jnp.sum(jnp.where(same, 1.0, 0.0), axis=1, keepdims=True)
     order = jnp.sum(jnp.where(same & (cols64 < rows64), 1.0, 0.0), axis=1, keepdims=True)
-    eye8 = (
-        lax.broadcasted_iota(jnp.int32, (TOP, TOP), 0) == lax.broadcasted_iota(jnp.int32, (TOP, TOP), 1)
-    ).astype(BF)
-    routes_t = lax.dot_general(eye8, routes[...].astype(BF), NT, preferred_element_type=F32)
-    pick_t = lax.dot_general(eye8, pick[...].astype(BF), NT, preferred_element_type=F32)
+    routes_t = routes[...].astype(F32)
+    pick_t = pick[...].astype(F32)
     hit = jnp.zeros((PL, TOK), F32)
     for k in range(TOP):
         route = routes_t[k : k + 1, :]
@@ -261,7 +257,7 @@
         wanted = jnp.where(copies == 1.0, 0.0, jnp.where(copies == 2.0, by2, by3))
         hit = hit + jnp.where((route == plc_col) & (wanted == order), 1.0, 0.0)
     names = (plc_col == lax.broadcasted_iota(jnp.int32, (PL, EXPERTS), 1).astype(F32)).astype(BF)
-    router_rows = lax.dot_general(names, router[...], NT, preferred_element_type=F32).astype(BF)
+    router_rows = jnp.dot(names, router[...], preferred_element_type=F32).astype(BF)
 
     for r in orings:
         r.arrive(3)
@@ -344,36 +340,26 @@
             for d2, k2 in hops:
                 events.append((k + k2 + 2, q, functools.partial(a2_arrive, q, label, aa, d2, k2)))
     events.sort(key=lambda ev: ev[:2])
-    for n, (_, _, run) in enumerate(events):
-        pump(22.5 + 0.42 * n)
-        run()
 
     lane32 = lax.broadcasted_iota(jnp.int32, (TOP, 32), 1)
     row32 = lax.broadcasted_iota(jnp.int32, (TOP, 32), 0)
     mine = SLOTS * chip + row32
     pick_lo = ((lane32 == mine) & (row32 < SLOTS)).astype(BF)
     pick_hi = ((lane32 + 32 == mine) & (row32 < SLOTS)).astype(BF)
-
-    def take_weights(s, carry):
-        table = xq[0, s, TOK : TOK + 32, :]
-        wt[pl.ds(pl.multiple_of(s * 8, 8), 8), :] = jnp.dot(
-            pick_lo, table[:, 0:128], preferred_element_type=F32
-        ) + jnp.dot(pick_hi, table[:, 128:256], preferred_element_type=F32)
-        return carry
-
-    lax.fori_loop(0, CHIPS, take_weights, 0)
-    weights = wt[0:128, :]
     rows128 = lax.broadcasted_iota(jnp.int32, (TOK, TOK), 0)
     cols128 = lax.broadcasted_iota(jnp.int32, (TOK, TOK), 1)
     earlier = (rows128 < cols128).astype(BF)
-    taken = weights > 0.0
-    rank = jnp.dot(taken.astype(BF), earlier, preferred_element_type=F32)
-    wt[pl.ds(128, 128), :] = jnp.where(taken, rank, -1.0)
-
-    def compact(s, carry):
-        base = pl.multiple_of(s * 8, 8)
-        w8 = wt[pl.ds(base, 8), :]
-        r8 = wt[pl.ds(pl.multiple_of(128 + s * 8, 8), 8), :]
+
+    def compact(where, n, carry):
+        dx, dy = where(lax.div(n, 2), lax.rem(n, 2))
+        s = wrap(x + dx, NX) * NY + wrap(y + dy, NY)
+        table = xq[0, s, TOK : TOK + 32, :]
+        w8 = jnp.dot(pick_lo, table[:, 0:128], preferred_element_type=F32) + jnp.dot(
+            pick_hi, table[:, 128:256], preferred_element_type=F32
+        )
+        taken = w8 > 0.0
+        rank = jnp.dot(jnp.where(taken, 1.0, 0.0).astype(BF), earlier, preferred_element_type=F32)
+        r8 = jnp.where(taken, rank, -1.0)
         rows = lax.broadcasted_iota(jnp.int32, (CAP, TOK), 0).astype(F32)
         here = [rows == r8[j : j + 1, :] for j in range(SLOTS)]
         chosen = jnp.concatenate([jnp.where(h, 1.0, 0.0) for h in here], axis=0).astype(BF)
@@ -386,9 +372,23 @@
             xc[j, pl.ds(pl.multiple_of(s * CAP, 16), CAP), :] = packed[j * CAP : (j + 1) * CAP, :]
         return carry
 
-    for g in range(4):
-        lax.fori_loop(g * 4, g * 4 + 4, compact, 0)
-        pump((45, 46, 50, 53)[g])
+    def compact_some(count, where):
+        lax.fori_loop(0, count, functools.partial(compact, where), 0)
+
+    ready = {
+        8: ((1, lambda h, m: (h, m)),),
+        24: ((4, lambda h, m: ((1 - h) * (1 + 2 * m), h * (1 + 2 * m))),),
+        44: ((2, lambda h, m: (2 * m, 2 - 2 * m)), (4, lambda h, m: (1 + 2 * h, 1 + 2 * m))),
+        58: ((4, lambda h, m: ((1 - h) * (1 + 2 * m) + 2 * h, h * (1 + 2 * m) + 2 - 2 * h)),),
+    }
+    for n, (_, _, run) in enumerate(events):
+        pump(22.5 + 0.38 * n)
+        run()
+        for group in ready.get(n, ()):
+            compact_some(*group)
+    pump(45)
+    compact_some(1, lambda h, m: (2 + h, 2 + m))
+    pump(53)
 
     def gate_up(c, n, carry):
         j = lax.div(n, 3)
@@ -560,7 +560,6 @@
             pltpu.VMEM((4, 3, 4, TOK, QW), BF),
             pltpu.VMEM((4, 3, TOK, QW), BF),
             pltpu.VMEM((TOK, D), BF),
-            pltpu.VMEM((256, TOK), F32),
             pltpu.VMEM((CHIPS, SLOTS * CAP, TOK), BF),
             dma((18,)),
             dma((2, 8)),
@@ -589,11 +588,11 @@
         output_weight,
         placed_gate_up,
         placed_down,
-        router,
+        router.T,
         norm_gain.reshape(1, D),
         final_gain.reshape(1, D),
-        routes,
-        replica_pick,
+        routes.T,
+        replica_pick.T,
         placement.reshape(1, PL),
     )
 

time: 131 us -> 128 us (0.977)
  local copies, waits for them, and re-layouts: 4.66 us -> 1.67 us
    unnamed x10 -> x1, local copies, waits for them, and re-layouts: 4.66 us -> 1.67 us
where the time goes in v3:
time: 128 us; the launch traced here: 127 us
  Pallas kernels  125 us (98%)
  local copies, waits for them, and re-layouts  1.67 us (1%)
    pallas_call x1, Pallas kernels, body(): pl.pallas_call(body_kernel, out_shape=jax.ShapeDtypeStruct((TOK, D), BF),...  125 us

profile of v3, /device:TPU:8, one launch (start us, length us, event | category | flops | bytes accessed | tf_op | source)
XLA Modules:
  0.0 127.0 jit_solution(9890730038150634796)
XLA Ops:
  0.0 125.3 %shard_map.109 = bf16[128,1024]{1,0:T(8,128)(2,1)} custom-call(bf16[128,1024]{1,0:T(8,128)(2,1)} %ho.1, bf16[128,1024]{1,0:T(8,128)(2,1)} %res.1, bf16[128,1024]{1,0:T(8,128)(2,1)} %wo_in.1, bf16[2,128,1024]{2,1,0:T(8,128)(2,1)} %gu_in.1, bf16[2,64,1024]{2,1,0:T(8,128)(2,1)} %dn_in.1, bf16[32,1024]{1,0:T(8,128)(2,1)} %bitcast.6, f32[1,1024]{1,0:T(1,128)} %bitcast.7, ...), custom_call_target="tpu_custom_call" | custom-call | tf_op jit(solution)/shard_map/pallas_call | solution.py:544
  125.3 1.7 %copy.13 = bf16[128,1024]{1,0:T(8,128)(2,1)} copy(bf16[128,1024]{1,0:T(8,128)(2,1)} %shard_map.109) | data formatting | bytes 524288

commit v4 on v3

--- a/solution.py
+++ b/solution.py
@@ -391,8 +391,8 @@
     pump(53)
 
     def gate_up(c, n, carry):
-        j = lax.div(n, 3)
-        at = pl.ds(pl.multiple_of(lax.rem(n, 3) * 256, 256), 256)
+        j = lax.div(n, 2)
+        at = pl.ds(pl.multiple_of(lax.rem(n, 2) * 384, 128), 384)
         both = jnp.dot(xc[j, at, :], wgu[c, j], preferred_element_type=F32)
         g, u = both[:, 0:HALF], both[:, HALF:]
         act[j, at, c * HALF : (c + 1) * HALF] = (g / (1.0 + jnp.exp(-g)) * u).astype(BF)
@@ -402,19 +402,17 @@
     for r in gu[0]:
         r.from_partner()
     for g in range(2):
-        lax.fori_loop(g * 6, g * 6 + 6, functools.partial(gate_up, 0), 0)
+        lax.fori_loop(g * 4, g * 4 + 4, functools.partial(gate_up, 0), 0)
         pump((57, 60)[g])
     for r in gu[1]:
         r.from_partner()
     for g in range(2):
-        lax.fori_loop(g * 6, g * 6 + 6, functools.partial(gate_up, 1), 0)
-        pump((62, 64)[g])
-
-    def down(h, n, carry):
-        j = lax.div(n, 3)
-        at = pl.ds(pl.multiple_of(lax.rem(n, 3) * 256, 256), 256)
-        out = jnp.dot(act[j, at, :], wd[h, j], preferred_element_type=F32)
-        yc[j, at, h * HW : (h + 1) * HW] = out.astype(BF)
+        lax.fori_loop(g * 4, g * 4 + 4, functools.partial(gate_up, 1), 0)
+        pump(62)
+
+    def down(h, j, carry):
+        out = jnp.dot(act[j], wd[h, j], preferred_element_type=F32)
+        yc[j, :, h * HW : (h + 1) * HW] = out.astype(BF)
         return carry
 
     def combine(h, s, carry):
@@ -503,8 +501,9 @@
     def produce(h):
         for r in dn[h]:
             r.from_partner()
-        lax.fori_loop(0, 12, functools.partial(down, h), 0)
-        lax.fori_loop(0, CHIPS, functools.partial(combine, h), 0)
+        lax.fori_loop(0, SLOTS, functools.partial(down, h), 0)
+        pump(64)
+        lax.fori_loop(0, CHIPS, functools.partial(combine, h), 0, unroll=4)
         s1_first(h)
         pump(68)
 

time: 128 us -> 122 us (0.953)
  Pallas kernels: 125 us -> 120 us
    pallas_call x1, Pallas kernels: 125 us -> 120 us  [body(): pl.pallas_call(body_kernel, out_shape=jax.ShapeDtypeStruct((TOK, D), BF),...]
where the time goes in v4:
time: 122 us
  Pallas kernels  120 us (98%)
  local copies, waits for them, and re-layouts  1.67 us (1%)
    pallas_call x1, Pallas kernels, body(): pl.pallas_call(body_kernel, out_shape=jax.ShapeDtypeStruct((TOK, D), BF),...  120 us

profile of v4, /device:TPU:8, one launch (start us, length us, event | category | flops | bytes accessed | tf_op | source)
XLA Modules:
  0.0 121.9 jit_solution(4092942905506118635)
XLA Ops:
  0.0 120.3 %shard_map.109 = bf16[128,1024]{1,0:T(8,128)(2,1)} custom-call(bf16[128,1024]{1,0:T(8,128)(2,1)} %ho.1, bf16[128,1024]{1,0:T(8,128)(2,1)} %res.1, bf16[128,1024]{1,0:T(8,128)(2,1)} %wo_in.1, bf16[2,128,1024]{2,1,0:T(8,128)(2,1)} %gu_in.1, bf16[2,64,1024]{2,1,0:T(8,128)(2,1)} %dn_in.1, bf16[32,1024]{1,0:T(8,128)(2,1)} %bitcast.6, f32[1,1024]{1,0:T(1,128)} %bitcast.7, ...), custom_call_target="tpu_custom_call" | custom-call | tf_op jit(solution)/shard_map/pallas_call | solution.py:543
  120.3 1.7 %copy.13 = bf16[128,1024]{1,0:T(8,128)(2,1)} copy(bf16[128,1024]{1,0:T(8,128)(2,1)} %shard_map.109) | data formatting | bytes 524288
